TPU v7x, 512 devices: a whole 4x4x16 slice. The times are simulated.
512 devices in a mesh: tm: 8 (over x, core), dp: 64 (over z, y).
Axes of the slice: x: 4, y: 4, z: 16, core: 2. Of those that a mesh axis runs over, the one named last changes fastest.
Arguments:
- edge_feat: bfloat16 [8, 8192, 186], P('tm', 'dp'), may hold values from -6 to 6
- endpoint_slots: int32 [8, 2, 8192], P('tm', None, 'dp'), may hold values from 0 to 2047, as said below
- neighbor_slots: int32 [8, 20, 8192], P('tm', None, 'dp'), may hold values from 0 to 2047, as said below
- neighbor_gap: int32 [8, 20, 8192], P('tm', None, 'dp'), may hold values from 0 to 999
- score_grad: float32 [8, 8192], P('tm', 'dp'), may hold values from -1.5 to 1.5
- node_list: int32 [8, 64, 2048], P('tm', 'dp'), may hold values from 0 to 128, as said below
- memory0: float32 [8192, 256], P('dp'), may hold values from -6 to 6
- msg_weight: bfloat16 [186, 256], replicated, may hold values from -0.4375 to 0.4375
- gate_weight: bfloat16 [256, 512], replicated, may hold values from -0.375 to 0.375
- gate_bias: float32 [512], replicated, may hold values from -4 to 4
- omega: float32 [256], replicated, may hold values from 0.001 to 1
- attn_weights: bfloat16 [4, 256, 256], replicated, may hold values from -0.375 to 0.375
- pred_weights: bfloat16 [2, 256, 256], replicated, may hold values from -0.375 to 0.375
- pred_out: float32 [256], replicated, may hold values from -0.375 to 0.375
Outputs:
- scores: float32 [8, 8192], P('tm', 'dp')
- new_memory: float32 [8, 8192, 256], P('tm', 'dp')
- grad_out_proj: float32 [256, 256], replicated
- grad_pred: float32 [2, 256, 256], replicated
Inputs may be any that keep to these rules, and one draw needn't show every extreme that they name: `node_list`: each block of 32 slots (one device's requests to one owner) holds distinct rows first and 128 in the empty slots after them; every block holds at least one row; in each mini-batch some owner's block is full from every device. `endpoint_slots`: every slot points at a non-empty entry of its device's node list. `neighbor_slots`: every slot points at a non-empty entry of its device's node list.
All inputs are finite; a program needn't handle non-finite values.
Results may differ from a plain program's by a relative error of at most 0.017.
Values may be sent and summed in bfloat16 or wider, within the bound.
No kernel may reach another device: no remote copies, remote signals or barrier semaphores. Data moves between devices by JAX's collectives and lax.ppermute only.
A program may use at most 64 MiB of HBM per device.

v0:
```python
import math
import jax
import jax.numpy as jnp
from jax import lax
from jax.sharding import PartitionSpec as P

HEADS = 2


def shifted(value, axis, steps):
    count = lax.axis_size(axis)
    initial, last = (max(0, -steps), min(count, count - steps))
    return lax.ppermute(value, axis, [(source, source + steps) for source in range(initial, last)])


def local_step(
    slot_rows,
    end_slots,
    near_slots,
    near_gaps,
    cot_rows,
    omega,
    attn_weights,
    pred_weights,
    pred_out,
):
    feat_width = slot_rows.shape[1]
    events = end_slots.shape[1]
    near_count = near_slots.shape[0] // 2
    head_dim = feat_width // HEADS
    self_rows = jnp.take(slot_rows, end_slots, axis=0)
    near_rows = jnp.take(slot_rows, near_slots, axis=0).reshape(2, near_count, events, feat_width)
    phases = near_gaps.reshape(2, near_count, events).astype(jnp.float32)[..., None] * omega
    near_feat = (near_rows.astype(jnp.float32) + jnp.cos(phases)).astype(jnp.bfloat16)
    query_proj = jnp.einsum(
        "pea,ab->peb", self_rows, attn_weights[0], preferred_element_type=jnp.float32
    )
    key_proj = jnp.einsum(
        "pkea,ab->pkeb", near_feat, attn_weights[1], preferred_element_type=jnp.float32
    )
    value_proj = jnp.einsum(
        "pkea,ab->pkeb", near_feat, attn_weights[2], preferred_element_type=jnp.float32
    )
    query_heads = query_proj.reshape(2, 1, events, HEADS, head_dim)
    key_heads = key_proj.reshape(2, near_count, events, HEADS, head_dim)
    value_heads = value_proj.reshape(2, near_count, events, HEADS, head_dim)
    att_logits = jnp.sum(query_heads * key_heads, axis=-1) / math.sqrt(head_dim)
    weights_att = jax.nn.softmax(att_logits, axis=1)
    mixed_heads = (
        jnp.sum(weights_att[..., None] * value_heads, axis=1)
        .reshape(2, events, feat_width)
        .astype(jnp.bfloat16)
    )
    state_full = self_rows.astype(jnp.float32) + jnp.einsum(
        "pea,ab->peb", mixed_heads, attn_weights[3], preferred_element_type=jnp.float32
    )
    state_bf = state_full.astype(jnp.bfloat16)
    pre_pred = jnp.dot(state_bf[0], pred_weights[0], preferred_element_type=jnp.float32) + jnp.dot(
        state_bf[1], pred_weights[1], preferred_element_type=jnp.float32
    )
    sigmoid_pre = jax.nn.sigmoid(pre_pred)
    logit_out = jnp.sum(pre_pred * sigmoid_pre * pred_out, axis=-1)
    grad_pre = (
        cot_rows[:, None] * pred_out * (sigmoid_pre * (1.0 + pre_pred * (1.0 - sigmoid_pre)))
    ).astype(jnp.bfloat16)
    grad_first = jnp.einsum("ea,eb->ab", state_bf[0], grad_pre, preferred_element_type=jnp.float32)
    grad_second = jnp.einsum("ea,eb->ab", state_bf[1], grad_pre, preferred_element_type=jnp.float32)
    grad_state = jnp.einsum(
        "eb,pab->pea", grad_pre, pred_weights, preferred_element_type=jnp.float32
    ).astype(jnp.bfloat16)
    grad_out_proj = jnp.einsum(
        "pea,peb->ab", mixed_heads, grad_state, preferred_element_type=jnp.float32
    )
    return (logit_out, grad_out_proj, jnp.stack([grad_first, grad_second]))


def per_device(
    edge_feat,
    endpoint_slots,
    neighbor_slots,
    neighbor_gap,
    score_grad,
    node_list,
    memory0,
    msg_weight,
    gate_weight,
    gate_bias,
    omega,
    attn_weights,
    pred_weights,
    pred_out,
):
    groups = lax.axis_size("dp")
    node_dev, feat_width = memory0.shape
    list_len = node_list.shape[2]
    per_owner = list_len // groups
    requests = node_list[0, 0].reshape(groups, per_owner)
    wanted = lax.all_to_all(requests, "dp", split_axis=0, concat_axis=0, tiled=True)
    message = jnp.dot(edge_feat[0], msg_weight, preferred_element_type=jnp.float32).astype(
        jnp.bfloat16
    )
    message_wide = message.astype(jnp.float32)
    end_slots = endpoint_slots[0]
    flat_ends = end_slots.reshape(-1)
    slot_sums = (
        jnp.zeros((list_len, feat_width), jnp.float32)
        .at[flat_ends]
        .add(jnp.concatenate([message_wide, message_wide]))
    )
    slot_tally = jnp.zeros((list_len,), jnp.float32).at[flat_ends].add(1.0)
    got_sums, got_tally = (
        lax.all_to_all(
            slot_sums.reshape(groups, per_owner, feat_width),
            "dp",
            split_axis=0,
            concat_axis=0,
            tiled=True,
        ),
        lax.all_to_all(
            slot_tally.reshape(groups, per_owner), "dp", split_axis=0, concat_axis=0, tiled=True
        ),
    )
    picker = (wanted.reshape(-1)[:, None] == jnp.arange(node_dev)[None, :]).astype(jnp.bfloat16)
    flat_sums = got_sums.reshape(-1, feat_width)
    sums_high = flat_sums.astype(jnp.bfloat16)
    sums_low = (flat_sums - sums_high.astype(jnp.float32)).astype(jnp.bfloat16)
    totals = jnp.einsum(
        "sn,sd->nd", picker, sums_high, preferred_element_type=jnp.float32
    ) + jnp.einsum("sn,sd->nd", picker, sums_low, preferred_element_type=jnp.float32)
    counts = jnp.dot(
        got_tally.reshape(-1), picker.astype(jnp.float32), precision=lax.Precision.HIGHEST
    )
    touched = (counts > 0.5).astype(jnp.float32)
    mean_msg = (totals / jnp.maximum(counts, 1.0)[:, None]).astype(jnp.bfloat16)
    pre_gate = jnp.dot(mean_msg, gate_weight, preferred_element_type=jnp.float32) + gate_bias
    update = jax.nn.sigmoid(pre_gate[:, :feat_width]) * touched[:, None]
    candidate = jnp.tanh(pre_gate[:, feat_width:])
    decay_rate = 1.0 - update
    inject = update * candidate
    section_index = lax.axis_index("tm")
    before = memory0
    for relay_step in range(lax.axis_size("tm") - 1):
        moved_state = shifted((decay_rate * before + inject).astype(jnp.bfloat16), "tm", 1).astype(
            jnp.float32
        )
        before = jnp.where(section_index == 0, memory0, moved_state)
    new_memory = decay_rate * before + inject
    memory_bf = before.astype(jnp.bfloat16)
    full_table = lax.all_gather(memory_bf, "dp", axis=0, tiled=True)
    owner_of = jnp.arange(list_len, dtype=jnp.int32) // per_owner
    global_row = owner_of * node_dev + jnp.minimum(node_list[0, 0], node_dev - 1)
    slot_rows = jnp.take(full_table, global_row, axis=0)
    logit_out, grad_out, grad_pair = local_step(
        slot_rows,
        end_slots,
        neighbor_slots[0],
        neighbor_gap[0],
        score_grad[0],
        omega,
        attn_weights,
        pred_weights,
        pred_out,
    )
    grad_out, grad_pair = lax.psum((grad_out, grad_pair), ("tm", "dp"))
    return (logit_out[None, :], new_memory[None], grad_out, grad_pair)


def solution(mesh):
    in_specs = (
        P("tm", "dp", None),
        P("tm", None, "dp"),
        P("tm", None, "dp"),
        P("tm", None, "dp"),
        P("tm", "dp"),
        P("tm", "dp", None),
        P("dp", None),
        P(),
        P(),
        P(),
        P(),
        P(),
        P(),
        P(),
    )
    out_specs = (P("tm", "dp"), P("tm", "dp", None), P(), P())
    return jax.shard_map(
        per_device, mesh=mesh, in_specs=in_specs, out_specs=out_specs, check_vma=False
    )
```

profile of v0, /device:TPU:2, one launch (start us, length us, event | category | flops | bytes accessed | tf_op | source)
XLA Modules:
  0.0 856.8 jit_solution(11601709572848172272)
XLA Ops:
  7.7 1.4 broadcast_minimum_fusion
  9.1 0.7 all_to_all.15
  9.8 18.7 %all-to-all-start = ((s32[64,1,32]{2,1,0:T(1,128)}), s32[64,1,32]{2,1,0:T(1,128)S(1)}, u32[]{:S(2)}, u32[]{:S(2)}) async-start(s32[64,1,32]{2,1,0:T(1,128)} %bitcast.2), calls=%async_computation | async-start | bytes 65536 | tf_op jit(solution)/shard_map/all_to_all | solution.py:98
  28.5 0.7 compare_select_fusion.4
  29.2 2.0 scatter_custom_fusion.1
  31.2 0.7 all_to_all.18
  31.8 11.2 %all-to-all-done = s32[64,1,32]{2,1,0:T(1,128)S(1)} async-done(((s32[64,1,32]{2,1,0:T(1,128)}), s32[64,1,32]{2,1,0:T(1,128)S(1)}, u32[]{:S(2)}, u32[]{:S(2)}) %all-to-all-start) | async-done | bytes 8224 | tf_op jit(solution)/shard_map/all_to_all | solution.py:98
  43.0 4.6 all-to-all-start.2
  47.6 1.1 convolution_convert_fusion.1
  48.7 3.4 scatter_custom_fusion
  52.1 10.2 %all-to-all-done.2 = f32[64,1,32]{2,1,0:T(1,128)S(1)} async-done(((f32[64,1,32]{2,1,0:T(1,128)}), f32[64,1,32]{2,1,0:T(1,128)S(1)}, u32[]{:S(2)}, u32[]{:S(2)}) %all-to-all-start.2) | async-done | bytes 8224 | tf_op jit(solution)/shard_map/all_to_all | solution.py:119
  62.3 4.9 all-to-all-start.1
  67.3 0.7 reduce.12
  68.6 0.7 reduce.13
  70.0 95.7 %all-to-all-done.1 = f32[64,32,256]{2,1,0:T(8,128)S(1)} async-done(((f32[64,32,256]{2,1,0:T(8,128)}), f32[64,32,256]{2,1,0:T(8,128)S(1)}, u32[]{:S(2)}, u32[]{:S(2)}) %all-to-all-start.1) | async-done | bytes 2097184 | tf_op jit(solution)/shard_map/all_to_all | solution.py:112
  166.0 0.8 fusion.7
  166.8 1.0 convolution_add_fusion.1
  168.0 2.1 collective-permute-start
  170.0 3.6 collective-permute-done
  173.8 1.9 collective-permute-start.1
  175.7 3.7 collective-permute-done.1
  179.5 2.1 collective-permute-start.2
  181.5 3.7 collective-permute-done.2
  185.3 1.9 collective-permute-start.3
  187.2 3.7 collective-permute-done.3
  191.0 1.9 collective-permute-start.4
  192.9 3.7 collective-permute-done.4
  196.7 1.9 collective-permute-start.5
  198.6 3.7 collective-permute-done.5
  202.3 1.9 collective-permute-start.6
  204.3 3.7 collective-permute-done.6
  207.9 0.6 fusion.30
  209.0 0.8 copy.39
  209.8 0.8 copy.40
  210.7 136.2 %all-gather.2.cloned.1.call-done = bf16[8192,256]{1,0:T(8,128)(2,1)} async-done(((bf16[128,256]{1,0:T(8,128)(2,1)}), bf16[8192,256]{1,0:T(8,128)(2,1)}) %all-gather.2.cloned.1.call-update) | async-done | bytes 4194320 | tf_op jit(solution)/shard_map/all_gather | solution.py:149
  346.9 9.4 %gather_fusion = bf16[2048,256]{1,0:T(8,128)(2,1)S(1)} fusion(bf16[8192,256]{1,0:T(8,128)(2,1)} %all-gather.2.cloned.1.call-done, s32[2048]{0:T(1024)S(1)} %broadcast_clamp_fusion), kind=kCustom, calls=%fused_computation | custom fusion | bytes 2105344 | tf_op jit(solution)/shard_map/jit(_take)/gather | solution.py:152
  356.7 7.6 gather_fusion.2
  364.3 1.2 gather_fusion.1
  365.8 10.1 %add_convert_fusion = bf16[20,128,256]{2,1,0:T(8,128)(2,1)S(1)} fusion(f32[256]{0:T(256)S(1)} %copy-done.10, f32[20,128]{1,0:T(8,128)S(1)} %bitcast.137, bf16[20,128,256]{2,1,0:T(8,128)(2,1)S(1)} %bitcast.127, pred[20,128]{1,0:T(8,128)(4,1)S(1)} %compare_and_fusion), kind=kLoop, calls=%fused_computation.7 | loop fusion | flops 3276800 | bytes 2635264 | tf_op jit(solution)/shard_map/convert_element_type | solution.py:34
  376.8 1.1 multiply_reduce_fusion
  378.1 1.1 fusion.1
  379.4 0.8 multiply_reduce_fusion.2
  380.7 1.1 convolution_bitcast_fusion.2
  381.8 0.8 pad_maximum_fusion
  382.6 0.7 add_bitcast_fusion
  383.4 463.0 %all-reduce.3.cloned.1.call-done = (f32[256,256]{1,0:T(8,128)}, f32[2,256,256]{2,1,0:T(8,128)}) async-done(((f32[256,256]{1,0:T(8,128)}, f32[2,256,256]{2,1,0:T(8,128)}), (f32[256,256]{1,0:T(8,128)}, f32[2,256,256]{2,1,0:T(8,128)})) %all-reduce.3.cloned.1.call-update) | async-done | bytes 786448 | tf_op jit(solution)/shard_map/psum | solution.py:164
  846.4 1.7 copy.58
  848.1 1.9 copy.59
  (70 shorter events, 5.6 us)
Async XLA Ops:
  7.2 159.7 %copy-start = (bf16[256,512]{1,0:T(8,128)(2,1)S(1)}, bf16[256,512]{1,0:T(8,128)(2,1)}, u32[]{:S(2)}) copy-start(bf16[256,512]{1,0:T(8,128)(2,1)} %param.22) | copy-start | bytes 786436
  9.8 33.3 %all-to-all-start = ((s32[64,1,32]{2,1,0:T(1,128)}), s32[64,1,32]{2,1,0:T(1,128)S(1)}, u32[]{:S(2)}, u32[]{:S(2)}) async-start(s32[64,1,32]{2,1,0:T(1,128)} %bitcast.2), calls=%async_computation | async-start | bytes 65536 | tf_op jit(solution)/shard_map/all_to_all | solution.py:98
  43.0 19.3 %all-to-all-start.2 = ((f32[64,1,32]{2,1,0:T(1,128)}), f32[64,1,32]{2,1,0:T(1,128)S(1)}, u32[]{:S(2)}, u32[]{:S(2)}) async-start(f32[64,1,32]{2,1,0:T(1,128)} %bitcast.8), calls=%async_computation.2 | async-start | bytes 65536 | tf_op jit(solution)/shard_map/all_to_all | solution.py:119
  62.3 103.4 %all-to-all-start.1 = ((f32[64,32,256]{2,1,0:T(8,128)}), f32[64,32,256]{2,1,0:T(8,128)S(1)}, u32[]{:S(2)}, u32[]{:S(2)}) async-start(f32[64,32,256]{2,1,0:T(8,128)} %bitcast.6), calls=%async_computation.1 | async-start | bytes 4194304 | tf_op jit(solution)/shard_map/all_to_all | solution.py:112
  67.2 279.7 %all-gather.2.cloned.1.call-start = ((), (), s32[]{:S(2)}) async-start(), calls=%async_computation.3 | async-start | bytes 4259840 | tf_op jit(solution)/shard_map/all_gather | solution.py:149
  70.0 96.8 %copy-start.11 = (f32[512]{0:T(512)S(1)}, f32[512]{0:T(512)}, u32[]{:S(2)}) copy-start(f32[512]{0:T(512)} %param.23) | copy-start | bytes 6148
  166.0 1.8 copy-start.1
  167.8 41.0 %copy-start.8 = (s32[1,20,128]{2,0,1:T(1,128)S(1)}, s32[1,20,128]{2,0,1:T(1,128)}, u32[]{:S(2)}) copy-start(s32[1,20,128]{2,0,1:T(1,128)} %param.17) | copy-start | bytes 30724
  167.8 41.0 %copy-start.2 = (bf16[4,256,256]{2,1,0:T(8,128)(2,1)S(1)}, bf16[4,256,256]{2,1,0:T(8,128)(2,1)}, u32[]{:S(2)}) copy-start(bf16[4,256,256]{2,1,0:T(8,128)(2,1)} %param.25) | copy-start | bytes 1572868
  168.0 5.7 collective-permute-start
  173.8 5.6 collective-permute-start.1
  179.4 31.1 %copy-start.9 = (s32[1,2,128]{2,1,0:T(2,128)S(1)}, s32[1,2,128]{2,1,0:T(2,128)}, u32[]{:S(2)}) copy-start(s32[1,2,128]{2,1,0:T(2,128)} %param.15) | copy-start | bytes 3076
  179.5 31.1 %copy-start.6 = (s32[1,20,128]{2,0,1:T(1,128)S(1)}, s32[1,20,128]{2,0,1:T(1,128)}, u32[]{:S(2)}) copy-start(s32[1,20,128]{2,0,1:T(1,128)} %param.16) | copy-start | bytes 30724
  179.5 31.2 %copy-start.7 = (s32[1,1,2048]{2,1,0:T(1,128)S(1)}, s32[1,1,2048]{2,1,0:T(1,128)}, u32[]{:S(2)}) copy-start(s32[1,1,2048]{2,1,0:T(1,128)} %param.19) | copy-start | bytes 24580
  179.5 5.7 collective-permute-start.2
  185.3 5.6 collective-permute-start.3
  191.0 5.6 collective-permute-start.4
  196.7 5.6 collective-permute-start.5
  202.3 5.6 collective-permute-start.6
  208.6 637.8 %all-reduce.3.cloned.1.call-start = ((), (), s32[]{:S(2)}) async-start(), calls=%async_computation.4 | async-start | bytes 1572864 | tf_op jit(solution)/shard_map/psum | solution.py:164
  356.7 9.0 %copy-start.10 = (f32[256]{0:T(256)S(1)}, f32[256]{0:T(256)}, u32[]{:S(2)}) copy-start(f32[256]{0:T(256)} %param.24) | copy-start | bytes 3076
  365.5 10.5 %copy-start.4 = (bf16[256,256]{1,0:T(8,128)(2,1)S(1)}, bf16[256,256]{1,0:T(8,128)(2,1)}, u32[]{:S(2)}) copy-start(bf16[256,256]{1,0:T(8,128)(2,1)} %copy.39) | copy-start | bytes 393220
  375.9 0.9 copy-start.3
  376.5 2.7 copy-start.5
  376.8 2.6 copy-start.12
  376.8 3.4 copy-start.13
Sparse Core Ops, SparseCore 0:
  208.7 138.1 all-gather.1
  382.8 463.6 all-reduce.2
where the time goes:
time: 858 us; the launch traced here: 857 us
  waiting for transfers between devices  742 us (86%)
  starting transfers between devices  42.2 us (5%)
  local copies, waits for them, and re-layouts  26.3 us (3%)
  other arithmetic  22.7 us (3%)
  between operations  14.6 us (2%)
  matrix products  9.08 us (1%)
    psum x1, waiting for transfers between devices, per_device(): grad_out, grad_pair = lax.psum((grad_out, grad_pair), ('tm', 'dp'))  463 us
    all_gather x1, waiting for transfers between devices, per_device(): full_table = lax.all_gather(memory_bf, 'dp', axis=0, tiled=True)  136 us
    all_to_all x1, waiting for transfers between devices, per_device(): lax.all_to_all(slot_sums.reshape(groups, per_owner, feat_width), 'dp', sp...  95.7 us
    ppermute x7, waiting for transfers between devices, shifted(): lax.ppermute(value, axis, [(source, source + steps) for source in range(i...  25.6 us
    all_to_all x1, starting transfers between devices, per_device(): lax.all_to_all(requests, 'dp', split_axis=0, concat_axis=0, tiled=True)  18.7 us
  transfers between devices with their start and end apart: 12, of which 12 were waited for; matrix products, arithmetic and copies ran while one was open for 1% of the time, Pallas kernels for 0%

commit v1 on v0

--- a/solution.py
+++ b/solution.py
@@ -146,7 +146,9 @@
         before = jnp.where(section_index == 0, memory0, moved_state)
     new_memory = decay_rate * before + inject
     memory_bf = before.astype(jnp.bfloat16)
-    full_table = lax.all_gather(memory_bf, "dp", axis=0, tiled=True)
+    full_table = jnp.concatenate(
+        lax.all_to_all(jnp.stack([memory_bf] * lax.axis_size("dp")), "dp", 0, 0), axis=0
+    )
     owner_of = jnp.arange(list_len, dtype=jnp.int32) // per_owner
     global_row = owner_of * node_dev + jnp.minimum(node_list[0, 0], node_dev - 1)
     slot_rows = jnp.take(full_table, global_row, axis=0)

time: 858 us -> 913 us (1.064)
  waiting for transfers between devices: 742 us -> 789 us
    all_to_all x0 -> x1, waiting for transfers between devices: none -> 187 us  [per_device(): lax.all_to_all(jnp.stack([memory_bf] * lax.axis_size('dp')), 'dp', 0, 0)]
    all_gather x1 -> x0, waiting for transfers between devices: 136 us -> none  [per_device(): full_table = lax.all_gather(memory_bf, 'dp', axis=0, tiled=True)]
where the time goes in v1:
time: 913 us; the launch traced here: 912 us
  waiting for transfers between devices  789 us (86%)
  starting transfers between devices  48.1 us (5%)
  local copies, waits for them, and re-layouts  28.7 us (3%)
  other arithmetic  22.1 us (2%)
  between operations  14.6 us (2%)
    psum x1, waiting for transfers between devices, per_device(): grad_out, grad_pair = lax.psum((grad_out, grad_pair), ('tm', 'dp'))  459 us
    all_to_all x1, waiting for transfers between devices, per_device(): lax.all_to_all(jnp.stack([memory_bf] * lax.axis_size('dp')), 'dp', 0, 0)  187 us
    all_to_all x1, waiting for transfers between devices, per_device(): lax.all_to_all(slot_sums.reshape(groups, per_owner, feat_width), 'dp', sp...  95.8 us
    ppermute x7, waiting for transfers between devices, shifted(): lax.ppermute(value, axis, [(source, source + steps) for source in range(i...  25.6 us
    all_to_all x1, starting transfers between devices, per_device(): lax.all_to_all(requests, 'dp', split_axis=0, concat_axis=0, tiled=True)  18.7 us
  transfers between devices with their start and end apart: 12, of which 12 were waited for; matrix products, arithmetic and copies ran while one was open for 1% of the time, Pallas kernels for 0%

profile of v1, /device:TPU:2, one launch (start us, length us, event | category | flops | bytes accessed | tf_op | source)
XLA Modules:
  0.0 912.0 jit_solution(10934504841420755870)
XLA Ops:
  7.7 1.4 broadcast_minimum_fusion
  9.1 0.7 all_to_all.18
  9.8 18.7 %all-to-all-start = ((s32[64,1,32]{2,1,0:T(1,128)}), s32[64,1,32]{2,1,0:T(1,128)S(1)}, u32[]{:S(2)}, u32[]{:S(2)}) async-start(s32[64,1,32]{2,1,0:T(1,128)} %bitcast.2), calls=%async_computation | async-start | bytes 65536 | tf_op jit(solution)/shard_map/all_to_all | solution.py:98
  29.2 2.0 scatter_custom_fusion.1
  31.2 0.7 all_to_all.21
  31.8 11.2 %all-to-all-done = s32[64,1,32]{2,1,0:T(1,128)S(1)} async-done(((s32[64,1,32]{2,1,0:T(1,128)}), s32[64,1,32]{2,1,0:T(1,128)S(1)}, u32[]{:S(2)}, u32[]{:S(2)}) %all-to-all-start) | async-done | bytes 8224 | tf_op jit(solution)/shard_map/all_to_all | solution.py:98
  43.0 4.6 all-to-all-start.2
  47.6 1.1 convolution_convert_fusion.1
  48.7 3.4 scatter_custom_fusion
  52.1 10.2 %all-to-all-done.2 = f32[64,1,32]{2,1,0:T(1,128)S(1)} async-done(((f32[64,1,32]{2,1,0:T(1,128)}), f32[64,1,32]{2,1,0:T(1,128)S(1)}, u32[]{:S(2)}, u32[]{:S(2)}) %all-to-all-start.2) | async-done | bytes 8224 | tf_op jit(solution)/shard_map/all_to_all | solution.py:119
  62.3 4.9 all-to-all-start.1
  67.2 0.7 reduce.12
  68.5 0.7 reduce.13
  70.0 95.8 %all-to-all-done.1 = f32[64,32,256]{2,1,0:T(8,128)S(1)} async-done(((f32[64,32,256]{2,1,0:T(8,128)}), f32[64,32,256]{2,1,0:T(8,128)S(1)}, u32[]{:S(2)}, u32[]{:S(2)}) %all-to-all-start.1) | async-done | bytes 2097184 | tf_op jit(solution)/shard_map/all_to_all | solution.py:112
  166.0 0.8 fusion.7
  166.8 1.0 convolution_add_fusion.1
  167.9 1.9 collective-permute-start
  169.9 3.6 collective-permute-done
  173.6 1.9 collective-permute-start.1
  175.5 3.7 collective-permute-done.1
  179.3 1.9 collective-permute-start.2
  181.2 3.7 collective-permute-done.2
  185.0 1.9 collective-permute-start.3
  186.9 3.7 collective-permute-done.3
  190.6 1.9 collective-permute-start.4
  192.6 3.7 collective-permute-done.4
  196.3 1.9 collective-permute-start.5
  198.2 3.7 collective-permute-done.5
  202.0 1.9 collective-permute-start.6
  203.9 3.7 collective-permute-done.6
  207.6 2.5 stack.8
  210.1 6.2 all-to-all-start.3
  216.8 0.8 copy.39
  217.5 0.8 copy.40
  218.5 187.2 %all-to-all-done.3 = bf16[64,128,256]{2,1,0:T(8,128)(2,1)} async-done(((bf16[64,128,256]{2,1,0:T(8,128)(2,1)}), bf16[64,128,256]{2,1,0:T(8,128)(2,1)}, u32[]{:S(2)}, u32[]{:S(2)}) %all-to-all-start.3) | async-done | bytes 4194336 | tf_op jit(solution)/shard_map/all_to_all | solution.py:150
  405.7 9.4 %gather_fusion = bf16[2048,256]{1,0:T(8,128)(2,1)S(1)} fusion(bf16[8192,256]{1,0:T(8,128)(2,1)} %bitcast.10, s32[2048]{0:T(1024)S(1)} %broadcast_clamp_fusion), kind=kCustom, calls=%fused_computation | custom fusion | bytes 2105344 | tf_op jit(solution)/shard_map/jit(_take)/gather | solution.py:154
  415.6 7.6 gather_fusion.2
  423.1 1.2 gather_fusion.1
  424.6 10.1 %add_convert_fusion = bf16[20,128,256]{2,1,0:T(8,128)(2,1)S(1)} fusion(f32[256]{0:T(256)S(1)} %copy-done.10, f32[20,128]{1,0:T(8,128)S(1)} %bitcast.138, bf16[20,128,256]{2,1,0:T(8,128)(2,1)S(1)} %bitcast.128, pred[20,128]{1,0:T(8,128)(4,1)S(1)} %compare_and_fusion), kind=kLoop, calls=%fused_computation.7 | loop fusion | flops 3276800 | bytes 2635264 | tf_op jit(solution)/shard_map/convert_element_type | solution.py:34
  435.6 1.1 multiply_reduce_fusion
  436.9 1.1 fusion.1
  438.2 0.8 multiply_reduce_fusion.2
  439.5 1.1 convolution_bitcast_fusion.2
  440.6 0.8 pad_maximum_fusion
  441.4 0.7 add_bitcast_fusion
  442.2 459.4 %all-reduce.3.cloned.1.call-done = (f32[256,256]{1,0:T(8,128)}, f32[2,256,256]{2,1,0:T(8,128)}) async-done(((f32[256,256]{1,0:T(8,128)}, f32[2,256,256]{2,1,0:T(8,128)}), (f32[256,256]{1,0:T(8,128)}, f32[2,256,256]{2,1,0:T(8,128)})) %all-reduce.3.cloned.1.call-update) | async-done | bytes 786448 | tf_op jit(solution)/shard_map/psum | solution.py:166
  901.6 1.7 copy.58
  903.3 1.9 copy.59
  (70 shorter events, 6.3 us)
Async XLA Ops:
  7.2 159.6 %copy-start = (bf16[256,512]{1,0:T(8,128)(2,1)S(1)}, bf16[256,512]{1,0:T(8,128)(2,1)}, u32[]{:S(2)}) copy-start(bf16[256,512]{1,0:T(8,128)(2,1)} %param.22) | copy-start | bytes 786436
  9.8 33.3 %all-to-all-start = ((s32[64,1,32]{2,1,0:T(1,128)}), s32[64,1,32]{2,1,0:T(1,128)S(1)}, u32[]{:S(2)}, u32[]{:S(2)}) async-start(s32[64,1,32]{2,1,0:T(1,128)} %bitcast.2), calls=%async_computation | async-start | bytes 65536 | tf_op jit(solution)/shard_map/all_to_all | solution.py:98
  43.0 19.3 %all-to-all-start.2 = ((f32[64,1,32]{2,1,0:T(1,128)}), f32[64,1,32]{2,1,0:T(1,128)S(1)}, u32[]{:S(2)}, u32[]{:S(2)}) async-start(f32[64,1,32]{2,1,0:T(1,128)} %bitcast.8), calls=%async_computation.2 | async-start | bytes 65536 | tf_op jit(solution)/shard_map/all_to_all | solution.py:119
  62.3 103.4 %all-to-all-start.1 = ((f32[64,32,256]{2,1,0:T(8,128)}), f32[64,32,256]{2,1,0:T(8,128)S(1)}, u32[]{:S(2)}, u32[]{:S(2)}) async-start(f32[64,32,256]{2,1,0:T(8,128)} %bitcast.6), calls=%async_computation.1 | async-start | bytes 4194304 | tf_op jit(solution)/shard_map/all_to_all | solution.py:112
  70.0 96.9 %copy-start.11 = (f32[512]{0:T(512)S(1)}, f32[512]{0:T(512)}, u32[]{:S(2)}) copy-start(f32[512]{0:T(512)} %param.23) | copy-start | bytes 6148
  166.0 1.8 copy-start.1
  167.9 5.6 collective-permute-start
  173.6 5.6 collective-permute-start.1
  179.3 5.6 collective-permute-start.2
  185.0 5.6 collective-permute-start.3
  190.6 5.6 collective-permute-start.4
  196.3 5.6 collective-permute-start.5
  202.0 5.6 collective-permute-start.6
  210.1 6.5 copy-start.8
  210.1 6.5 copy-start.2
  210.1 8.2 copy-start.9
  210.1 8.2 copy-start.6
  210.1 8.3 copy-start.7
  210.1 195.6 %all-to-all-start.3 = ((bf16[64,128,256]{2,1,0:T(8,128)(2,1)}), bf16[64,128,256]{2,1,0:T(8,128)(2,1)}, u32[]{:S(2)}, u32[]{:S(2)}) async-start(bf16[64,128,256]{2,1,0:T(8,128)(2,1)} %stack.8), calls=%async_computation.3 | async-start | bytes 8388608 | tf_op jit(solution)/shard_map/all_to_all | solution.py:150
  216.3 685.2 %all-reduce.3.cloned.1.call-start = ((), (), s32[]{:S(2)}) async-start(), calls=%async_computation.4 | async-start | bytes 1572864 | tf_op jit(solution)/shard_map/psum | solution.py:166
  415.5 9.0 copy-start.10
  424.3 10.5 %copy-start.4 = (bf16[256,256]{1,0:T(8,128)(2,1)S(1)}, bf16[256,256]{1,0:T(8,128)(2,1)}, u32[]{:S(2)}) copy-start(bf16[256,256]{1,0:T(8,128)(2,1)} %copy.39) | copy-start | bytes 393220
  434.7 0.9 copy-start.3
  435.3 2.7 copy-start.5
  435.6 2.5 copy-start.12
  435.6 3.4 copy-start.13
Sparse Core Ops, SparseCore 0:
  441.6 459.9 all-reduce.2
